TPU v7x, 32 devices: a whole 2x2x4 slice. The times are simulated.
32 devices in a mesh: wl: 4 (over x, core), row: 4 (over z), col: 2 (over y).
Axes of the slice: x: 2, y: 2, z: 4, core: 2. Of those that a mesh axis runs over, the one named last changes fastest.
Arguments:
- cotangent: bfloat16 [4, 2, 4096, 4096], P('wl', None, 'row', 'col'), may hold values from -6 to 6
- incident: bfloat16 [4, 4096, 4096], P('wl', 'row', 'col'), may hold values from 0.5 to 1.5
- aperture_tiles: int32 [32, 32], P('row', 'col'), may hold values 0 or 1
- charge: int32 [4], P('wl'), may hold values from 2 to 8
- wl_index: int32 [4], P('wl'), may hold values from 0 to 16
Outputs:
- gradient: bfloat16 [4096, 4096], P('row', 'col')
All inputs are finite; a program needn't handle non-finite values. No bound on the sum of `aperture_tiles` on one device may be relied on, other than what follows from the above.
Results may differ from a plain program's by a relative error of at most 0.013.
Values may be sent and summed in bfloat16 or wider, within the bound.
No kernel may reach another device: no remote copies, remote signals or barrier semaphores. Data moves between devices by JAX's collectives and lax.ppermute only.
A program may use at most 128 MiB of HBM per device.

v0:
```python
import math
import jax
import jax.numpy as jnp
from jax import lax
from jax.sharding import PartitionSpec as P

M = 512


def phase_grid(offset, amount, extent, size_m, index_value, transpose):
    pupil_pos = 2 * (offset + jnp.arange(amount, dtype=jnp.int32)) - extent + 1
    focal_pos = 2 * jnp.arange(size_m, dtype=jnp.int32) - size_m + 1
    if transpose:
        product = focal_pos[:, None] * pupil_pos[None, :]
    else:
        product = pupil_pos[:, None] * focal_pos[None, :]
    period = size_m * (32 + index_value)
    remainder = jnp.remainder(4 * product, period)
    return remainder.astype(jnp.float32) * (jnp.float32(2.0 * math.pi) / period.astype(jnp.float32))


def vortex(focal_re, focal_im, charge_value):
    size_m = focal_re.shape[1]
    row_count = focal_re.shape[0]
    row_pos = (2 * jnp.arange(row_count, dtype=jnp.int32) - size_m + 1).astype(jnp.float32)
    col_pos = (2 * jnp.arange(size_m, dtype=jnp.int32) - size_m + 1).astype(jnp.float32)
    angles = jnp.arctan2(col_pos[None, :], row_pos[:, None]) * charge_value.astype(jnp.float32)
    cosine = jnp.cos(angles)
    sine_value = jnp.sin(angles)
    turned_re = focal_re * cosine + focal_im * sine_value
    turned_im = focal_im * cosine - focal_re * sine_value
    return jnp.concatenate([turned_re, turned_im], axis=1).astype(jnp.bfloat16)


def per_device(cotangent, incident, aperture_tiles, charge, wl_index):
    rows_local = cotangent.shape[2]
    cols_local = cotangent.shape[3]
    row_first = lax.axis_index("row") * rows_local
    col_first = lax.axis_index("col") * cols_local
    extent = rows_local * lax.axis_size("row")
    size_m = M
    tile_rows = aperture_tiles.shape[0]
    tile_cols = aperture_tiles.shape[1]
    tile_size = rows_local // tile_rows
    open_tiles = (aperture_tiles == 1).astype(jnp.bfloat16)
    live_cells = jnp.broadcast_to(
        open_tiles[:, None, :, None], (tile_rows, tile_size, tile_cols, tile_size)
    ).reshape(rows_local, cols_local)
    wave_index = wl_index[0]
    norm_fwd = 1.0 / math.sqrt(extent)
    norm_back = 1.0 / math.sqrt(size_m)
    contract_first = (((0,), (0,)), ((), ()))
    col_phase = phase_grid(col_first, cols_local, extent, size_m, wave_index, False)
    fwd_cols = (
        jnp.concatenate([jnp.cos(col_phase), jnp.sin(col_phase)], axis=1) * norm_fwd
    ).astype(jnp.bfloat16)
    grad_re = cotangent[0, 0] * live_cells
    grad_im = cotangent[0, 1] * live_cells
    prod_re = jnp.dot(grad_re, fwd_cols, preferred_element_type=jnp.float32)
    prod_im = jnp.dot(grad_im, fwd_cols, preferred_element_type=jnp.float32)
    inner = jnp.concatenate(
        [prod_re[:, :size_m] - prod_im[:, size_m:], prod_re[:, size_m:] + prod_im[:, :size_m]],
        axis=1,
    ).astype(jnp.bfloat16)
    row_phase = phase_grid(row_first, rows_local, extent, size_m, wave_index, False)
    row_cos = jnp.cos(row_phase)
    row_sin = jnp.sin(row_phase)
    fwd_rcos = (row_cos * norm_fwd).astype(jnp.bfloat16)
    fwd_rsin = (row_sin * norm_fwd).astype(jnp.bfloat16)
    back_rcos = (row_cos * norm_back).astype(jnp.bfloat16)
    back_rsin = (row_sin * norm_back).astype(jnp.bfloat16)
    cos_part = fwd_rcos
    sin_part = fwd_rsin
    with_cos = lax.dot_general(cos_part, inner, contract_first, preferred_element_type=jnp.float32)
    with_sin = lax.dot_general(sin_part, inner, contract_first, preferred_element_type=jnp.float32)
    shared = lax.psum(
        jnp.concatenate(
            [
                with_cos[:, :size_m] - with_sin[:, size_m:],
                with_cos[:, size_m:] + with_sin[:, :size_m],
            ],
            axis=1,
        ),
        ("row", "col"),
    )
    turned = vortex(shared[:, :size_m], shared[:, size_m:], charge[0])
    cos_part = back_rcos
    sin_part = back_rsin
    first_part = jnp.dot(cos_part, turned, preferred_element_type=jnp.float32)
    second_part = jnp.dot(sin_part, turned, preferred_element_type=jnp.float32)
    pupil_focal = jnp.concatenate(
        [
            first_part[:, :size_m] + second_part[:, size_m:],
            first_part[:, size_m:] - second_part[:, :size_m],
        ],
        axis=1,
    )
    back_y = pupil_focal.astype(jnp.bfloat16)
    col_back = phase_grid(col_first, cols_local, extent, size_m, wave_index, True)
    back_cols = (
        jnp.concatenate([jnp.cos(col_back), jnp.sin(col_back)], axis=0) * norm_back
    ).astype(jnp.bfloat16)
    back_real = jnp.dot(back_y, back_cols, preferred_element_type=jnp.float32)
    wave_term = (
        back_real * incident[0].astype(jnp.float32) * live_cells.astype(jnp.float32)
    ).astype(jnp.bfloat16)
    summed = lax.psum(wave_term, "wl").astype(jnp.float32)
    return summed.astype(jnp.bfloat16)


def solution(mesh):
    return jax.shard_map(
        per_device,
        mesh=mesh,
        in_specs=(
            P("wl", None, "row", "col"),
            P("wl", "row", "col"),
            P("row", "col"),
            P("wl"),
            P("wl"),
        ),
        out_specs=P("row", "col"),
        check_vma=False,
    )
```

profile of v0, /device:TPU:0, one launch (start us, length us, event | category | flops | bytes accessed | tf_op | source)
XLA Modules:
  0.0 437.1 jit_solution(7436106996927162927)
XLA Ops:
  6.5 0.0 all-reduce.3.cloned.1.call-start
  7.2 0.7 compare_convert_fusion
  8.0 64.3 %fusion.22 = (f32[2048,512]{1,0:T(8,128)S(1)}, f32[2048,512]{1,0:T(8,128)S(1)}) fusion(f32[]{:T(128)S(6)} %div.2, s32[]{:T(128)S(6)} %select_n.21, s32[512]{0:T(512)S(1)} %multiply_add_fusion.2, s32[2048]{0:T(1024)S(1)} %multiply_add_fusion, pred[]{:T(512)S(6)} %lt.21), kind=kLoop, calls=%fused_computation.30 | loop fusion | flops 11534336 | bytes 8398857 | tf_op jit(solution)/shard_map/cos | solution.py:55
  72.3 0.6 broadcast_in_dim.2
  72.9 0.0 copy-start
  72.9 10.3 %fusion.9 = f32[1024,1024]{0,1:T(8,128)} fusion(bf16[1,2,1024,2048]{3,2,1,0:T(8,128)(2,1)} %param.5, bf16[128,8,16,128]{3,2,1,0:T(8,128)(2,1)S(1)} %bitcast.23, f32[2048,512]{1,0:T(8,128)S(1)} %get-tuple-element.14, f32[2048,512]{1,0:T(8,128)S(1)} %get-tuple-element.13), kind=kOutput, calls=%fused_computation.15 | convolution fusion | flops 4303355904 | bytes 20971520 | tf_op jit(solution)/shard_map/dot_general | solution.py:59
  83.3 0.0 copy-done
  83.3 8.9 %fusion.10 = f32[1024,1024]{0,1:T(8,128)} fusion(bf16[1,2,1024,2048]{3,2,1,0:T(8,128)(2,1)} %param.5, bf16[128,8,16,128]{3,2,1,0:T(8,128)(2,1)S(1)} %bitcast.24, f32[2048,512]{1,0:T(8,128)S(1)} %get-tuple-element.14, f32[2048,512]{1,0:T(8,128)S(1)} %get-tuple-element.13), kind=kOutput, calls=%fused_computation.16 | convolution fusion | flops 4303355904 | bytes 20971520 | tf_op jit(solution)/shard_map/dot_general | solution.py:60
  92.2 4.2 fusion.35
  96.4 28.7 %fusion.46 = f32[512,1024]{1,0:T(8,128)S(1)} fusion(bf16[1024,512]{0,1:T(8,128)(2,1)S(1)} %get-tuple-element.8, bf16[1024,512]{0,1:T(8,128)(2,1)S(1)} %get-tuple-element.7, f32[]{:T(128)S(6)} %div.2, s32[]{:T(128)S(6)} %select_n.21, s32[512]{0:T(512)S(1)} %multiply_add_fusion.2, s32[1024]{0:T(1024)S(1)} %multiply_add_fusion.1, pred[]{:T(512)S(6)} %lt.21), kind=kOutput, calls=%fused_computation.66 | convolution fusion | flops 1084751872 | bytes 4200457 | tf_op jit(solution)/shard_map/dot_general | solution.py:74
  125.0 28.5 %fusion.45 = f32[512,1024]{1,0:T(8,128)S(1)} fusion(bf16[1024,512]{0,1:T(8,128)(2,1)S(1)} %get-tuple-element.8, bf16[1024,512]{0,1:T(8,128)(2,1)S(1)} %get-tuple-element.7, f32[]{:T(128)S(6)} %div.2, s32[]{:T(128)S(6)} %select_n.21, s32[512]{0:T(512)S(1)} %multiply_add_fusion.2, s32[1024]{0:T(1024)S(1)} %multiply_add_fusion.1, pred[]{:T(512)S(6)} %lt.21), kind=kOutput, calls=%fused_computation.65 | convolution fusion | flops 1084751872 | bytes 4200457 | tf_op jit(solution)/shard_map/dot_general | solution.py:75
  153.6 0.5 slice_subtract_fusion.2
  154.1 1.5 pad_maximum_fusion.1
  155.5 0.0 all-reduce.3.cloned.1.call-update
  155.6 0.0 all-reduce.5.cloned.1.call-start
  156.3 58.1 %fusion.17 = (f32[512,2048]{1,0:T(8,128)}, f32[512,2048]{1,0:T(8,128)}) fusion(f32[]{:T(128)S(6)} %div.2, s32[]{:T(128)S(6)} %select_n.21, s32[2048]{0:T(1024)S(1)} %multiply_add_fusion, s32[512]{0:T(512)S(1)} %multiply_add_fusion.2, pred[]{:T(512)S(6)} %lt.21), kind=kLoop, calls=%fused_computation.24 | loop fusion | flops 11534336 | bytes 8398857 | tf_op jit(solution)/shard_map/cos | solution.py:101
  214.3 46.3 %all-reduce.3.cloned.1.call-done = f32[512,1024]{1,0:T(8,128)} async-done(((f32[512,1024]{1,0:T(8,128)}), f32[512,1024]{1,0:T(8,128)}) %all-reduce.3.cloned.1.call-update) | async-done | bytes 2097168 | tf_op jit(solution)/shard_map/psum | solution.py:76
  260.6 8.1 %add_convert_fusion = (bf16[512,512]{1,0:T(8,128)(2,1)S(1)}, bf16[512,512]{1,0:T(8,128)(2,1)S(1)}) fusion(f32[512,1024]{1,0:T(8,128)} %all-reduce.3.cloned.1.call-done, f32[]{:T(128)} %bitcast.3, f32[512]{0:T(512)S(1)} %fusion.81), kind=kLoop, calls=%fused_computation.73 | loop fusion | flops 2359296 | bytes 3149828 | tf_op jit(solution)/shard_map/convert.3
  268.7 28.2 %fusion.47 = f32[1024,1024]{0,1:T(8,128)S(1)} fusion(f32[]{:T(128)S(6)} %div.2, s32[]{:T(128)S(6)} %select_n.21, s32[512]{0:T(512)S(1)} %multiply_add_fusion.2, s32[1024]{0:T(1024)S(1)} %multiply_add_fusion.1, pred[]{:T(512)S(6)} %lt.21, bf16[512,512]{1,0:T(8,128)(2,1)S(1)} %get-tuple-element.12, bf16[512,512]{1,0:T(8,128)(2,1)S(1)} %get-tuple-element.11), kind=kOutput, calls=%fused_computation.67 | convolution fusion | flops 1082654720 | bytes 5249033 | tf_op jit(solution)/shard_map/dot_general | solution.py:89
  297.0 0.0 copy-start.3
  297.0 28.5 %fusion.48 = f32[1024,1024]{0,1:T(8,128)S(1)} fusion(f32[]{:T(128)S(6)} %div.2, s32[]{:T(128)S(6)} %select_n.21, s32[512]{0:T(512)S(1)} %multiply_add_fusion.2, s32[1024]{0:T(1024)S(1)} %multiply_add_fusion.1, pred[]{:T(512)S(6)} %lt.21, bf16[512,512]{1,0:T(8,128)(2,1)S(1)} %get-tuple-element.12, bf16[512,512]{1,0:T(8,128)(2,1)S(1)} %get-tuple-element.11), kind=kOutput, calls=%fused_computation.68 | convolution fusion | flops 1082654720 | bytes 5249033 | tf_op jit(solution)/shard_map/dot_general | solution.py:90
  325.4 0.0 copy-start.1
  325.5 0.0 copy-start.2
  325.5 2.1 fusion.33
  327.6 0.0 copy-done.3
  327.6 0.8 copy-done.1
  328.4 1.3 copy-done.2
  329.7 10.6 %fusion.3 = bf16[1024,2048]{1,0:T(8,128)(2,1)} fusion(f32[512,2048]{1,0:T(8,128)S(1)} %copy-done.3, f32[512,2048]{1,0:T(8,128)S(1)} %copy-done.2, bf16[1,1024,2048]{2,1,0:T(8,128)(2,1)} %param.6, bf16[128,8,16,128]{3,2,1,0:T(8,128)(2,1)S(1)} %bitcast.25, bf16[1024,512]{0,1:T(8,128)(2,1)} %get-tuple-element.6, bf16[1024,512]{0,1:T(8,128)(2,1)} %get-tuple-element.5), kind=kOutput, calls=%fused_computation.6 | convolution fusion | flops 4315938816 | bytes 23068672 | tf_op jit(solution)/shard_map/dot_general | solution.py:103
  340.3 0.0 all-reduce.5.cloned.1.call-update
  340.3 84.9 %all-reduce.5.cloned.1.call-done = bf16[1024,2048]{1,0:T(8,128)(2,1)} async-done(((bf16[1024,2048]{1,0:T(8,128)(2,1)}), bf16[1024,2048]{1,0:T(8,128)(2,1)}) %all-reduce.5.cloned.1.call-update) | async-done | bytes 4194320 | tf_op jit(solution)/shard_map/psum | solution.py:107
  425.2 4.8 %copy.20 = bf16[1024,2048]{1,0:T(8,128)(2,1)} copy(bf16[1024,2048]{1,0:T(8,128)(2,1)} %all-reduce.5.cloned.1.call-done) | data formatting | bytes 8388608
  (4 shorter events, 0.0 us)
Async XLA Ops:
  6.5 254.1 %all-reduce.3.cloned.1.call-start = ((), (), s32[]{:S(2)}) async-start(), calls=%async_computation | async-start | bytes 4194304 | tf_op jit(solution)/shard_map/psum | solution.py:76
  72.9 10.4 %copy-start = (bf16[8,128,16,128]{3,2,1,0:T(8,128)(2,1)}, bf16[8,128,16,128]{3,2,1,0:T(8,128)(2,1)S(1)}, u32[]{:S(2)}) copy-start(bf16[8,128,16,128]{3,2,1,0:T(8,128)(2,1)S(1)} %broadcast_in_dim.2) | copy-start | bytes 12582916
  155.6 269.7 %all-reduce.5.cloned.1.call-start = ((), (), s32[]{:S(2)}) async-start(), calls=%async_computation.1 | async-start | bytes 8388608 | tf_op jit(solution)/shard_map/psum | solution.py:107
  297.0 30.6 %copy-start.3 = (f32[512,2048]{1,0:T(8,128)S(1)}, f32[512,2048]{1,0:T(8,128)}, u32[]{:S(2)}) copy-start(f32[512,2048]{1,0:T(8,128)} %get-tuple-element.16) | copy-start | bytes 12582916
  325.4 2.9 copy-start.1
  325.5 4.2 copy-start.2
Sparse Core Ops, SparseCore 0:
  155.7 104.9 all-reduce.2
  340.4 84.7 all-reduce.4
where the time goes:
time: 438 us; the launch traced here: 437 us
  matrix products  144 us (33%)
  other arithmetic  140 us (32%)
  waiting for transfers between devices  131 us (30%)
  between operations  15.2 us (3%)
  local copies, waits for them, and re-layouts  7.49 us (2%)
    psum x1, waiting for transfers between devices, per_device(): summed = lax.psum(wave_term, 'wl').astype(jnp.float32)  84.9 us
    cos x1, other arithmetic, per_device(): jnp.cos(col_phase)  64.3 us
    cos x1, other arithmetic, per_device(): jnp.cos(col_back)  58.1 us
    psum x1, waiting for transfers between devices, per_device(): lax.psum(jnp.concatenate([with_cos[:, :size_m] - with_sin[:, size_m:], wi...  46.3 us
    dot_general x1, matrix products, per_device(): lax.dot_general(cos_part, inner, contract_first, preferred_element_type=j...  28.7 us
    dot_general x1, matrix products, per_device(): lax.dot_general(sin_part, inner, contract_first, preferred_element_type=j...  28.5 us
    dot_general x1, matrix products, per_device(): second_part = jnp.dot(sin_part, turned, preferred_element_type=jnp.float32)  28.5 us
    dot_general x1, matrix products, per_device(): first_part = jnp.dot(cos_part, turned, preferred_element_type=jnp.float32)  28.2 us
  transfers between devices with their start and end apart: 2, of which 2 were waited for; matrix products, arithmetic and copies ran while one was open for 13% of the time, Pallas kernels for 0%

commit v1 on v0

--- a/solution.py
+++ b/solution.py
@@ -74,14 +74,17 @@
     with_cos = lax.dot_general(cos_part, inner, contract_first, preferred_element_type=jnp.float32)
     with_sin = lax.dot_general(sin_part, inner, contract_first, preferred_element_type=jnp.float32)
     shared = lax.psum(
-        jnp.concatenate(
-            [
-                with_cos[:, :size_m] - with_sin[:, size_m:],
-                with_cos[:, size_m:] + with_sin[:, :size_m],
-            ],
-            axis=1,
+        lax.psum(
+            jnp.concatenate(
+                [
+                    with_cos[:, :size_m] - with_sin[:, size_m:],
+                    with_cos[:, size_m:] + with_sin[:, :size_m],
+                ],
+                axis=1,
+            ),
+            "col",
         ),
-        ("row", "col"),
+        "row",
     )
     turned = vortex(shared[:, :size_m], shared[:, size_m:], charge[0])
     cos_part = back_rcos

time: 438 us -> 486 us (1.11)
  waiting for transfers between devices: 131 us -> 180 us
    psum x0 -> x1, waiting for transfers between devices: none -> 29.7 us  [per_device(): lax.psum(lax.psum(jnp.concatenate([with_cos[:, :size_m] - with_sin[:, siz...]
    psum x1, waiting for transfers between devices: 46.3 us -> 65.8 us  [per_device(): lax.psum(jnp.concatenate([with_cos[:, :size_m] - with_sin[:, size_m:], wi...]
  transfers between devices with their start and end apart: 2 -> 3, of which waited for: 2 -> 3; matrix products, arithmetic and copies ran while one was open for 13% -> 12% of each run, Pallas kernels for 0% -> 0%
where the time goes in v1:
time: 486 us
  waiting for transfers between devices  180 us (37%)
  matrix products  144 us (30%)
  other arithmetic  139 us (29%)
  between operations  14.9 us (3%)
  local copies, waits for them, and re-layouts  7.49 us (2%)
    psum x1, waiting for transfers between devices, per_device(): summed = lax.psum(wave_term, 'wl').astype(jnp.float32)  84.7 us
    psum x1, waiting for transfers between devices, per_device(): lax.psum(jnp.concatenate([with_cos[:, :size_m] - with_sin[:, size_m:], wi...  65.8 us
    cos x1, other arithmetic, per_device(): jnp.cos(col_phase)  64.3 us
    cos x1, other arithmetic, per_device(): jnp.cos(col_back)  58.1 us
    psum x1, waiting for transfers between devices, per_device(): lax.psum(lax.psum(jnp.concatenate([with_cos[:, :size_m] - with_sin[:, siz...  29.7 us
    dot_general x1, matrix products, per_device(): lax.dot_general(cos_part, inner, contract_first, preferred_element_type=j...  28.7 us
    dot_general x1, matrix products, per_device(): lax.dot_general(sin_part, inner, contract_first, preferred_element_type=j...  28.5 us
    dot_general x1, matrix products, per_device(): second_part = jnp.dot(sin_part, turned, preferred_element_type=jnp.float32)  28.5 us
  transfers between devices with their start and end apart: 3, of which 3 were waited for; matrix products, arithmetic and copies ran while one was open for 12% of the time, Pallas kernels for 0%

profile of v1, /device:TPU:0, one launch (start us, length us, event | category | flops | bytes accessed | tf_op | source)
XLA Modules:
  0.0 485.9 jit_solution(1383664181652944255)
XLA Ops:
  6.5 0.0 all-reduce.4.cloned.1.call-start
  7.2 0.7 compare_convert_fusion
  8.0 64.3 %fusion.22 = (f32[2048,512]{1,0:T(8,128)S(1)}, f32[2048,512]{1,0:T(8,128)S(1)}) fusion(f32[]{:T(128)S(6)} %div.2, s32[]{:T(128)S(6)} %select_n.21, s32[512]{0:T(512)S(1)} %multiply_add_fusion.2, s32[2048]{0:T(1024)S(1)} %multiply_add_fusion, pred[]{:T(512)S(6)} %lt.21), kind=kLoop, calls=%fused_computation.30 | loop fusion | flops 11534336 | bytes 8398857 | tf_op jit(solution)/shard_map/cos | solution.py:55
  72.3 0.6 broadcast_in_dim.2
  72.9 10.3 %fusion.9 = f32[1024,1024]{0,1:T(8,128)} fusion(bf16[1,2,1024,2048]{3,2,1,0:T(8,128)(2,1)} %param.5, bf16[128,8,16,128]{3,2,1,0:T(8,128)(2,1)S(1)} %bitcast.23, f32[2048,512]{1,0:T(8,128)S(1)} %get-tuple-element.14, f32[2048,512]{1,0:T(8,128)S(1)} %get-tuple-element.13), kind=kOutput, calls=%fused_computation.15 | convolution fusion | flops 4303355904 | bytes 20971520 | tf_op jit(solution)/shard_map/dot_general | solution.py:59
  83.3 0.0 copy-done
  83.3 8.9 %fusion.10 = f32[1024,1024]{0,1:T(8,128)} fusion(bf16[1,2,1024,2048]{3,2,1,0:T(8,128)(2,1)} %param.5, bf16[128,8,16,128]{3,2,1,0:T(8,128)(2,1)S(1)} %bitcast.24, f32[2048,512]{1,0:T(8,128)S(1)} %get-tuple-element.14, f32[2048,512]{1,0:T(8,128)S(1)} %get-tuple-element.13), kind=kOutput, calls=%fused_computation.16 | convolution fusion | flops 4303355904 | bytes 20971520 | tf_op jit(solution)/shard_map/dot_general | solution.py:60
  92.2 4.2 fusion.35
  96.4 28.7 %fusion.46 = f32[512,1024]{1,0:T(8,128)S(1)} fusion(bf16[1024,512]{0,1:T(8,128)(2,1)S(1)} %get-tuple-element.8, bf16[1024,512]{0,1:T(8,128)(2,1)S(1)} %get-tuple-element.7, f32[]{:T(128)S(6)} %div.2, s32[]{:T(128)S(6)} %select_n.21, s32[512]{0:T(512)S(1)} %multiply_add_fusion.2, s32[1024]{0:T(1024)S(1)} %multiply_add_fusion.1, pred[]{:T(512)S(6)} %lt.21), kind=kOutput, calls=%fused_computation.66 | convolution fusion | flops 1084751872 | bytes 4200457 | tf_op jit(solution)/shard_map/dot_general | solution.py:74
  125.0 28.5 %fusion.45 = f32[512,1024]{1,0:T(8,128)S(1)} fusion(bf16[1024,512]{0,1:T(8,128)(2,1)S(1)} %get-tuple-element.8, bf16[1024,512]{0,1:T(8,128)(2,1)S(1)} %get-tuple-element.7, f32[]{:T(128)S(6)} %div.2, s32[]{:T(128)S(6)} %select_n.21, s32[512]{0:T(512)S(1)} %multiply_add_fusion.2, s32[1024]{0:T(1024)S(1)} %multiply_add_fusion.1, pred[]{:T(512)S(6)} %lt.21), kind=kOutput, calls=%fused_computation.65 | convolution fusion | flops 1084751872 | bytes 4200457 | tf_op jit(solution)/shard_map/dot_general | solution.py:75
  153.6 0.5 slice_subtract_fusion.2
  154.1 1.5 pad_maximum_fusion.1
  155.5 0.0 all-reduce.4.cloned.1.call-update
  155.5 0.0 all-reduce.6.cloned.1.call-start
  155.6 65.8 %all-reduce.4.cloned.1.call-done = f32[512,1024]{1,0:T(8,128)} async-done(((f32[512,1024]{1,0:T(8,128)}), f32[512,1024]{1,0:T(8,128)}) %all-reduce.4.cloned.1.call-update) | async-done | bytes 2097168 | tf_op jit(solution)/shard_map/psum | solution.py:77
  221.4 0.0 all-reduce.6.cloned.1.call-update
  221.4 0.0 all-reduce.8.cloned.1.call-start
  222.1 58.1 %fusion.17 = (f32[512,2048]{1,0:T(8,128)}, f32[512,2048]{1,0:T(8,128)}) fusion(f32[]{:T(128)S(6)} %div.2, s32[]{:T(128)S(6)} %select_n.21, s32[2048]{0:T(1024)S(1)} %multiply_add_fusion, s32[512]{0:T(512)S(1)} %multiply_add_fusion.2, pred[]{:T(512)S(6)} %lt.21), kind=kLoop, calls=%fused_computation.24 | loop fusion | flops 11534336 | bytes 8398857 | tf_op jit(solution)/shard_map/cos | solution.py:104
  280.2 29.7 %all-reduce.6.cloned.1.call-done = f32[512,1024]{1,0:T(8,128)} async-done(((f32[512,1024]{1,0:T(8,128)}), f32[512,1024]{1,0:T(8,128)}) %all-reduce.6.cloned.1.call-update) | async-done | bytes 2097168 | tf_op jit(solution)/shard_map/psum | solution.py:76
  309.9 8.1 %add_convert_fusion = (bf16[512,512]{1,0:T(8,128)(2,1)S(1)}, bf16[512,512]{1,0:T(8,128)(2,1)S(1)}) fusion(f32[512,1024]{1,0:T(8,128)} %all-reduce.6.cloned.1.call-done, f32[]{:T(128)} %bitcast.3, f32[512]{0:T(512)S(1)} %fusion.81), kind=kLoop, calls=%fused_computation.73 | loop fusion | flops 2359296 | bytes 3149828 | tf_op jit(solution)/shard_map/convert.3
  318.1 28.2 %fusion.47 = f32[1024,1024]{0,1:T(8,128)S(1)} fusion(f32[]{:T(128)S(6)} %div.2, s32[]{:T(128)S(6)} %select_n.21, s32[512]{0:T(512)S(1)} %multiply_add_fusion.2, s32[1024]{0:T(1024)S(1)} %multiply_add_fusion.1, pred[]{:T(512)S(6)} %lt.21, bf16[512,512]{1,0:T(8,128)(2,1)S(1)} %get-tuple-element.12, bf16[512,512]{1,0:T(8,128)(2,1)S(1)} %get-tuple-element.11), kind=kOutput, calls=%fused_computation.67 | convolution fusion | flops 1082654720 | bytes 5249033 | tf_op jit(solution)/shard_map/dot_general | solution.py:92
  346.3 0.0 copy-start.3
  346.3 28.5 %fusion.48 = f32[1024,1024]{0,1:T(8,128)S(1)} fusion(f32[]{:T(128)S(6)} %div.2, s32[]{:T(128)S(6)} %select_n.21, s32[512]{0:T(512)S(1)} %multiply_add_fusion.2, s32[1024]{0:T(1024)S(1)} %multiply_add_fusion.1, pred[]{:T(512)S(6)} %lt.21, bf16[512,512]{1,0:T(8,128)(2,1)S(1)} %get-tuple-element.12, bf16[512,512]{1,0:T(8,128)(2,1)S(1)} %get-tuple-element.11), kind=kOutput, calls=%fused_computation.68 | convolution fusion | flops 1082654720 | bytes 5249033 | tf_op jit(solution)/shard_map/dot_general | solution.py:93
  374.8 0.0 copy-start.2
  374.8 2.1 fusion.33
  376.9 0.0 copy-done.3
  376.9 0.8 copy-done.1
  377.7 1.3 copy-done.2
  379.0 10.6 %fusion.3 = bf16[1024,2048]{1,0:T(8,128)(2,1)} fusion(f32[512,2048]{1,0:T(8,128)S(1)} %copy-done.3, f32[512,2048]{1,0:T(8,128)S(1)} %copy-done.2, bf16[1,1024,2048]{2,1,0:T(8,128)(2,1)} %param.6, bf16[128,8,16,128]{3,2,1,0:T(8,128)(2,1)S(1)} %bitcast.25, bf16[1024,512]{0,1:T(8,128)(2,1)} %get-tuple-element.6, bf16[1024,512]{0,1:T(8,128)(2,1)} %get-tuple-element.5), kind=kOutput, calls=%fused_computation.6 | convolution fusion | flops 4315938816 | bytes 23068672 | tf_op jit(solution)/shard_map/dot_general | solution.py:106
  389.6 0.0 all-reduce.8.cloned.1.call-update
  389.6 84.7 %all-reduce.8.cloned.1.call-done = bf16[1024,2048]{1,0:T(8,128)(2,1)} async-done(((bf16[1024,2048]{1,0:T(8,128)(2,1)}), bf16[1024,2048]{1,0:T(8,128)(2,1)}) %all-reduce.8.cloned.1.call-update) | async-done | bytes 4194320 | tf_op jit(solution)/shard_map/psum | solution.py:110
  474.3 4.8 copy.21
  (6 shorter events, 0.0 us)
Async XLA Ops:
  6.5 214.9 %all-reduce.4.cloned.1.call-start = ((), (), s32[]{:S(2)}) async-start(), calls=%async_computation | async-start | bytes 4194304 | tf_op jit(solution)/shard_map/psum | solution.py:77
  72.9 10.4 %copy-start = (bf16[8,128,16,128]{3,2,1,0:T(8,128)(2,1)}, bf16[8,128,16,128]{3,2,1,0:T(8,128)(2,1)S(1)}, u32[]{:S(2)}) copy-start(bf16[8,128,16,128]{3,2,1,0:T(8,128)(2,1)S(1)} %broadcast_in_dim.2) | copy-start | bytes 12582916
  155.5 154.4 %all-reduce.6.cloned.1.call-start = ((), (), s32[]{:S(2)}) async-start(), calls=%async_computation.1 | async-start | bytes 4194304 | tf_op jit(solution)/shard_map/psum | solution.py:76
  221.4 252.9 %all-reduce.8.cloned.1.call-start = ((), (), s32[]{:S(2)}) async-start(), calls=%async_computation.2 | async-start | bytes 8388608 | tf_op jit(solution)/shard_map/psum | solution.py:110
  346.3 30.6 %copy-start.3 = (f32[512,2048]{1,0:T(8,128)S(1)}, f32[512,2048]{1,0:T(8,128)}, u32[]{:S(2)}) copy-start(f32[512,2048]{1,0:T(8,128)} %get-tuple-element.16) | copy-start | bytes 12582916
  374.8 2.9 copy-start.1
  374.8 4.2 copy-start.2
Sparse Core Ops, SparseCore 0:
  155.7 65.6 all-reduce.3
  223.7 86.1 all-reduce.5
  389.7 84.5 all-reduce.7
